TPU v7x, 512 devices: a whole 4x8x8 slice. The times are simulated.
512 devices in a mesh: tile: 32 (over x, y), depth: 16 (over z, core).
Axes of the slice: x: 4, y: 8, z: 8, core: 2. Of those that a mesh axis runs over, the one named last changes fastest.
Arguments:
- coefficients: float32 [8, 16, 32, 128, 128], P(None, 'depth', 'tile'), may hold values from -24 to 24
- keep_count: int32 [16, 32, 128, 128], P('depth', 'tile'), may hold values from 1 to 8, as said below
- view_flip: int32 [32], P('tile'), may hold values from 0 to 1
Outputs:
- image: float32 [4, 512, 512], P(None, 'tile', 'depth')
Inputs may be any that keep to these rules, and one draw needn't show every extreme that they name: `keep_count`: along the block rows, blocks 2 j and 2 j + 1 of every brick and block column retain 8 + 1 slots together.
All inputs are finite; a program needn't handle non-finite values.
Results may differ from a plain program's by a relative error of at most 0.0003.
Values sent between devices are 32-bit elements; how exact they have to be, the bound alone decides.
A program may use at most 64 MiB of HBM per device.

v0:
```python
import math

import jax
import jax.numpy as jnp
import numpy as np
from jax import lax
from jax.sharding import PartitionSpec as P

slot_frequencies = (
    (0, 0, 0),
    (0, 0, 1),
    (0, 1, 0),
    (1, 0, 0),
    (0, 0, 2),
    (0, 1, 1),
    (0, 2, 0),
    (1, 0, 1),
)


def cosine_rows():
    result = np.zeros((4, 4))
    for frequency in range(4):
        factor = 0.5 if frequency == 0 else math.sqrt(0.5)
        for position in range(4):
            result[frequency, position] = factor * math.cos(
                math.pi * (2 * position + 1) * frequency / 8.0
            )
    return result


def basis_matrix(slot_count):
    rows_table = cosine_rows()
    result = np.zeros((4, 4, 4, slot_count))
    for slot_index in range(slot_count):
        freq_z, freq_x, freq_y = slot_frequencies[slot_index]
        result[:, :, :, slot_index] = (
            rows_table[freq_z][:, None, None]
            * rows_table[freq_x][None, :, None]
            * rows_table[freq_y][None, None, :]
        )
    return jnp.asarray(result.reshape(64, slot_count), dtype=jnp.float32)


def render_columns(block_coef, basis_rows, flipped, sample_count):
    slot_count, zblocks, column_count = block_coef.shape
    flat_coef = block_coef.reshape(slot_count, zblocks * column_count)
    cell_values = jnp.dot(
        basis_rows, flat_coef, precision=lax.Precision.HIGHEST, preferred_element_type=jnp.float32
    )
    cell_values = cell_values.reshape(4, 16, zblocks, column_count)
    density = jnp.transpose(cell_values, (2, 0, 1, 3)).reshape(zblocks * 4, 16, column_count)
    optical = 1.5 * jax.nn.softplus(2.0 * density) / sample_count
    inclusive = jnp.cumsum(optical, axis=0)
    total_depth = inclusive[-1]
    entering = jnp.where(flipped > 0, total_depth[None] - inclusive, inclusive - optical)
    weights = jnp.exp(-entering) * -jnp.expm1(-optical)
    red_sum = jnp.sum(weights * jax.nn.sigmoid(2.0 * density), axis=0)
    green_sum = jnp.sum(weights * jnp.exp(-density * density), axis=0)
    blue_sum = jnp.sum(weights * jax.nn.sigmoid(1.5 - density), axis=0)
    opacity = -jnp.expm1(-total_depth)
    return jnp.stack([red_sum, green_sum, blue_sum, opacity])


def to_image(layer, strip_blocks, column_blocks):
    spread = layer.reshape(4, 4, 4, strip_blocks, column_blocks)
    return jnp.transpose(spread, (0, 3, 1, 4, 2)).reshape(4, strip_blocks * 4, column_blocks * 4)


def composite(layers, flipped, layer_axis):
    clearance = 1.0 - layers[3:4]
    piece_count = layers.shape[layer_axis]
    forward = jnp.cumprod(clearance, axis=layer_axis)
    backward = jnp.flip(jnp.cumprod(jnp.flip(clearance, layer_axis), axis=layer_axis), layer_axis)
    unit_slice = jnp.ones_like(lax.slice_in_dim(clearance, 0, 1, axis=layer_axis))
    before_forward = jnp.concatenate(
        [unit_slice, lax.slice_in_dim(forward, 0, piece_count - 1, axis=layer_axis)],
        axis=layer_axis,
    )
    before_backward = jnp.concatenate(
        [lax.slice_in_dim(backward, 1, piece_count, axis=layer_axis), unit_slice], axis=layer_axis
    )
    passing = jnp.where(flipped > 0, before_backward, before_forward)
    return jnp.sum(passing * layers, axis=layer_axis)


def per_device(coefficients, keep_count, view_flip):
    slot_count = coefficients.shape[0]
    tile_count = lax.axis_size("tile")
    depth_count = lax.axis_size("depth")
    column_blocks = coefficients.shape[4]
    local_columns = coefficients.shape[3]
    strip_blocks = local_columns // tile_count
    flipped = view_flip[0]
    basis_rows = basis_matrix(slot_count)
    sample_count = 4 * tile_count * depth_count
    slot_index = lax.broadcasted_iota(jnp.int32, coefficients.shape, 0)
    masked = jnp.where(slot_index < keep_count[None], coefficients, jnp.float32(0.0))
    outgoing = masked.reshape(slot_count, 1, tile_count, strip_blocks * column_blocks)
    layer = render_columns(
        lax.all_to_all(outgoing, "tile", split_axis=2, concat_axis=1, tiled=True)[:, :, 0, :],
        basis_rows,
        flipped,
        sample_count,
    )
    picture = to_image(layer, strip_blocks, column_blocks)
    strip_width = picture.shape[1]
    band_rows = picture.shape[2] // depth_count
    pieces = picture.reshape(4, strip_width, depth_count, band_rows)
    gathered = lax.all_to_all(pieces, "depth", split_axis=2, concat_axis=2, tiled=True)
    return composite(gathered, flipped, 2)


def solution(mesh):
    placed = (P(None, "depth", "tile", None, None), P("depth", "tile", None, None), P("tile"))
    return jax.shard_map(
        per_device, mesh=mesh, in_specs=placed, out_specs=P(None, "tile", "depth"), check_vma=False
    )
```

profile of v0, /device:TPU:1, one launch (start us, length us, event | category | flops | bytes accessed | tf_op | source)
XLA Modules:
  0.0 85.6 jit_solution(12441692980066501912)
XLA Ops:
  0.0 1.1 %fusion.20 = f32[8,1,1,128,128]{4,3,2,1,0:T(8,128)S(1)} fusion(f32[8,1,1,128,128]{4,3,2,1,0:T(8,128)} %param.4, s32[128,128]{1,0:T(8,128)} %bitcast.113), kind=kLoop, calls=%fused_computation.29 | loop fusion | flops 262144 | bytes 1114112 | tf_op jit(solution)/shard_map/jit(_where)/select_n | solution.py:98
  1.1 0.1 reshape.37
  1.2 1.1 %copy.29 = f32[8,1,32,512]{3,0,1,2:T(8,128)} copy(f32[8,1,32,512]{3,2,0,1:T(8,128)S(1)} %reshape.37) | data formatting | bytes 1048576 | tf_op jit(solution)/shard_map/reshape | solution.py:99
  2.3 10.5 %all-to-all-start = ((f32[8,1,32,512]{3,0,1,2:T(8,128)}), f32[8,1,32,512]{3,0,1,2:T(8,128)S(1)}, u32[]{:S(2)}, u32[]{:S(2)}) async-start(f32[8,1,32,512]{3,0,1,2:T(8,128)} %copy.29), calls=%async_computation | async-start | bytes 1048576 | tf_op jit(solution)/shard_map/all_to_all | solution.py:101
  13.4 13.9 %all-to-all-done = f32[8,1,32,512]{3,0,1,2:T(8,128)S(1)} async-done(((f32[8,1,32,512]{3,0,1,2:T(8,128)}), f32[8,1,32,512]{3,0,1,2:T(8,128)S(1)}, u32[]{:S(2)}, u32[]{:S(2)}) %all-to-all-start) | async-done | bytes 524320 | tf_op jit(solution)/shard_map/all_to_all | solution.py:101
  27.3 3.4 %fusion.33 = f32[64,16384]{1,0:T(8,128)S(1)} fusion(f32[64,8]{1,0:T(8,128)S(1)} %copy-done.1, f32[8,16384]{1,0:T(8,128)S(1)} %bitcast.111), kind=kOutput, calls=%fused_computation.47 | convolution fusion | flops 100663296 | bytes 4720640 | tf_op jit(solution)/shard_map/dot_general | solution.py:48
  30.7 2.4 %copy.37 = f32[8,8,32,512]{3,2,1,0:T(8,128)S(1)} copy(f32[8,8,32,512]{3,1,2,0:T(8,128)S(1)} %bitcast.107) | data formatting | bytes 8388608
  33.1 0.0 copy-start
  33.1 0.9 %fusion.8 = f32[32,4,16,512]{3,0,2,1:T(8,128)S(1)} fusion(f32[4,16,32,512]{3,2,1,0:T(8,128)S(1)} %bitcast.105), kind=kLoop, calls=%fused_computation.11 | loop fusion | flops 1048576 | bytes 8388608 | tf_op jit(solution)/shard_map/mul | solution.py:53
  34.0 1.4 %copy-done = f32[8,8,32,512]{3,2,1,0:T(8,128)} copy-done((f32[8,8,32,512]{3,2,1,0:T(8,128)}, f32[8,8,32,512]{3,2,1,0:T(8,128)S(1)}, u32[]{:S(2)}) %copy-start) | copy-done | bytes 4194328
  35.4 2.4 %copy.30 = f32[32,4,16,512]{3,2,1,0:T(8,128)S(1)} copy(f32[32,4,16,512]{3,0,2,1:T(8,128)S(1)} %fusion.8) | data formatting | bytes 8388608 | tf_op jit(solution)/shard_map/mul | solution.py:53
  37.8 1.9 %fusion.14 = f32[128,16,512]{2,1,0:T(8,128)S(1)} fusion(f32[32,4,16,512]{3,2,1,0:T(8,128)S(1)} %copy.30), kind=kLoop, calls=%fused_computation.19 | loop fusion | flops 4194304 | bytes 8388608 | tf_op jit(solution)/shard_map/jit(softplus)/add | solution.py:53
  39.8 2.5 %fusion.4 = f32[128,16,512]{2,1,0:T(8,128)} fusion(f32[128,16,512]{2,1,0:T(8,128)S(1)} %bitcast.104, f32[128,16,512]{2,1,0:T(8,128)S(1)} %fusion.14), kind=kOutput, calls=%fused_computation.7 | output fusion | flops 136314880 | bytes 12582912 | tf_op jit(solution)/shard_map/jit(cumsum)/reduce_window_sum | solution.py:54
  42.3 0.8 slice_bitcast_fusion
  43.1 11.3 %multiply_reduce_fusion = (f32[16,512]{1,0:T(8,128)S(1)}, f32[16,512]{1,0:T(8,128)S(1)}, f32[16,512]{1,0:T(8,128)S(1)}) fusion(f32[32,4,16,512]{3,2,1,0:T(8,128)} %bitcast.108, f32[16,512]{1,0:T(8,128)S(1)} %get-tuple-element.8, pred[]{:T(512)} %bitcast, f32[4,16,32,512]{3,2,1,0:T(8,128)} %bitcast.106), kind=kLoop, calls=%fused_computation.23 | loop fusion | flops 31432704 | bytes 8519681 | tf_op jit(solution)/shard_map/reduce_sum | solution.py:58
  54.5 2.6 %copy.33 = f32[4,4,4,128,4]{4,3,2,1,0:T(8,128)} copy(f32[4,4,4,128,4]{3,1,4,2,0:T(4,128)S(1)} %maximum_bitcast_fusion) | data formatting | bytes 262144 | tf_op jit(solution)/shard_map/transpose | solution.py:67
  57.1 3.2 %reshape_reshape.3 = f32[4,16,16,32]{3,2,1,0:T(8,128)S(1)} reshape(f32[4,4,4,128,4]{4,3,2,1,0:T(8,128)} %copy.33) | data formatting | bytes 262144 | tf_op jit(solution)/shard_map/reshape;reshape | solution.py:109
  60.4 0.2 copy.46
  60.6 0.3 reshape.39
  60.8 22.1 %all_to_all.14 = f32[16,1,2048]{2,1,0:T(1,128)S(1)} all-to-all(f32[16,1,2048]{2,1,0:T(1,128)S(1)} %reshape.39), channel_id=1, replica_groups=mesh['tile'=32,'depth'=16] {'depth'}, dimensions={0} | all-to-all | bytes 262144 | tf_op jit(solution)/shard_map/all_to_all | solution.py:110
  83.0 0.6 broadcast.63
  83.5 1.0 %reduce.3 = f32[16,2048]{1,0:T(8,128)S(1)} reduce(f32[16,1,2048]{2,1,0:T(1,128)S(1)} %all_to_all.14, f32[]{:T(128)} %broadcast.63), dimensions={1}, to_apply=%all_to_all.5.reduce_sub_computation | reduce | bytes 262148 | tf_op jit(solution)/shard_map/all_to_all | solution.py:110
  84.5 0.2 reshape.40
  84.9 0.7 multiply_reduce_fusion.1
  (15 shorter events, 0.2 us)
Async XLA Ops:
  0.0 27.3 %copy-start.1 = (f32[64,8]{1,0:T(8,128)S(1)}, f32[64,8]{1,0:T(8,128)}, u32[]{:S(2)}) copy-start(f32[64,8]{1,0:T(8,128)} %constant.28.clone) | copy-start | bytes 6148
  2.3 25.0 %all-to-all-start = ((f32[8,1,32,512]{3,0,1,2:T(8,128)}), f32[8,1,32,512]{3,0,1,2:T(8,128)S(1)}, u32[]{:S(2)}, u32[]{:S(2)}) async-start(f32[8,1,32,512]{3,0,1,2:T(8,128)} %copy.29), calls=%async_computation | async-start | bytes 1048576 | tf_op jit(solution)/shard_map/all_to_all | solution.py:101
  33.1 2.3 %copy-start = (f32[8,8,32,512]{3,2,1,0:T(8,128)}, f32[8,8,32,512]{3,2,1,0:T(8,128)S(1)}, u32[]{:S(2)}) copy-start(f32[8,8,32,512]{3,2,1,0:T(8,128)S(1)} %copy.37) | copy-start | bytes 12582916
where the time goes:
time: 86.2 us; the launch traced here: 85.6 us
  blocking collectives  22.1 us (26%)
  other arithmetic  20.3 us (24%)
  local copies, waits for them, and re-layouts  14.6 us (17%)
  waiting for transfers between devices  13.9 us (16%)
  starting transfers between devices  10.5 us (12%)
  matrix products  3.38 us (4%)
    all_to_all x1, blocking collectives, per_device(): lax.all_to_all(pieces, 'depth', split_axis=2, concat_axis=2, tiled=True)  22.1 us
    all_to_all x1, waiting for transfers between devices, per_device(): lax.all_to_all(outgoing, 'tile', split_axis=2, concat_axis=1, tiled=True)  13.9 us
    reduce_sum x1, other arithmetic, render_columns(): red_sum = jnp.sum(weights * jax.nn.sigmoid(2.0 * density), axis=0)  11.3 us
    all_to_all x1, starting transfers between devices, per_device(): lax.all_to_all(outgoing, 'tile', split_axis=2, concat_axis=1, tiled=True)  10.5 us
    unnamed x7, local copies, waits for them, and re-layouts  4.22 us
    another operation x2, local copies, waits for them, and re-layouts, per_device(): pieces = picture.reshape(4, strip_width, depth_count, band_rows)  3.41 us
    dot_general x1, matrix products, render_columns(): jnp.dot(basis_rows, flat_coef, precision=lax.Precision.HIGHEST, preferred...  3.38 us
    transpose x1, local copies, waits for them, and re-layouts, to_image(): jnp.transpose(spread, (0, 3, 1, 4, 2))  2.62 us
  transfers between devices with their start and end apart: 1, of which 1 were waited for; matrix products, arithmetic and copies ran while one was open for 0% of the time, Pallas kernels for 0%

commit v1 on v0

v1 whole, which is shorter than its diff:
```python
import functools
import math

import jax
import jax.numpy as jnp
from jax import lax
from jax.experimental import pallas as pl
from jax.experimental.pallas import tpu as pltpu
from jax.sharding import PartitionSpec as P

MESH = pl.DeviceIdType.MESH
LOG2E = math.log2(math.e)


def cosine(frequency, position):
    factor = 0.5 if frequency == 0 else math.sqrt(0.5)
    return factor * math.cos(math.pi * (2 * position + 1) * frequency / 8.0)


def pack_strips(coef_ref, keep_ref, send_ref):
    lane_even = lax.broadcasted_iota(jnp.int32, (8, 128), 1) % 2 == 0
    row_low = lax.broadcasted_iota(jnp.int32, (8, 128), 0) % 4 < 2
    for group in range(16):
        rows = slice(8 * group, 8 * group + 8)
        count = keep_ref[rows, :]
        first = [coef_ref[k, rows, :] for k in range(8)]
        second = [pltpu.roll(value, 127, 1) for value in first]
        packed = [first[0]]
        packed += [jnp.where(count > k, first[k], second[8 - k]) for k in range(1, 8)]
        packed += [second[0], count.astype(jnp.float32)]
        for q in range(5):
            low, high = packed[2 * q], packed[2 * q + 1]
            own = jnp.where(row_low, low, pltpu.roll(high, 2, 0))
            other = jnp.where(row_low, pltpu.roll(low, 6, 0), high)
            merged = jnp.where(lane_even, own, pltpu.roll(other, 1, 1))
            send_ref[2 * group, q] = merged[0:4]
            send_ref[2 * group + 1, q] = merged[4:8]


def unpack_blocks(i, recv_ref, slots_ref):
    row_low = lax.broadcasted_iota(jnp.int32, (8, 128), 0) % 4 < 2
    tiles = [jnp.concatenate([recv_ref[i, q], recv_ref[16 + i, q]], axis=0) for q in range(5)]
    down = [pltpu.roll(value, 2, 0) for value in tiles]
    up = [pltpu.roll(value, 6, 0) for value in tiles]
    count = jnp.where(row_low, up[4], tiles[4])
    kept = jnp.where(row_low, count, 9.0 - count)
    for k in range(8):
        if k % 2 == 0:
            value = jnp.where(row_low, tiles[k // 2], down[(8 - k) // 2])
        else:
            value = jnp.where(row_low, up[k // 2], tiles[(7 - k) // 2])
        if k > 0:
            value = jnp.where(kept > k, value, 0.0)
        slots_ref[i, k] = value


def shade(density, state, sample_count):
    opacity, red, green, blue = state
    u = jnp.exp2(density)
    third = u * (LOG2E - u * (LOG2E / 2 - u * (LOG2E / 3)))
    soft = jnp.where(u < 2.0**-8, third, jnp.log2(1.0 + u))
    t = 1.5 * math.log(2.0) / sample_count
    alpha = soft * (t - soft * (t**2 / 2 - soft * (t**3 / 6 - soft * (t**4 / 24))))
    weight = (1.0 - opacity) * alpha
    v = jnp.exp2(0.5 * density - 1.5 * LOG2E)
    red = red + weight * jnp.exp2(density - soft)
    green = green + weight * jnp.exp2(density * density * (-1.0 / (4 * LOG2E)))
    blue = blue + weight * jnp.exp2(-jnp.log2(1.0 + v))
    return opacity + weight, red, green, blue


def render(x, flip, slots_ref, picture_ref, sample_count):
    unit = 2 * LOG2E
    c0 = cosine(0, 0)
    b1x, b2x = cosine(1, x), cosine(2, x)
    p, q, h = cosine(1, 0), cosine(1, 1), cosine(2, 0)
    turn = (1 - 2 * flip).astype(jnp.float32)

    def step(i, states):
        at = i + flip * (15 - 2 * i)
        a = [slots_ref[at, k] for k in range(8)]
        base = (unit * c0**3) * a[0] + (unit * c0**2 * b1x) * a[2] + (unit * c0**2 * b2x) * a[6]
        along = (unit * c0**2) * a[1] + (unit * c0 * b1x) * a[5]
        curve = (unit * c0**2 * h) * a[4]
        deep, tilt = (unit * c0**2 * turn) * a[3], (unit * c0 * turn) * a[7]
        outer, inner = base + curve, base - curve
        plane = [outer + p * along, inner + q * along, inner - q * along, outer - p * along]
        slope = [deep + p * tilt, deep + q * tilt, deep - q * tilt, deep - p * tilt]
        result = []
        for y in range(4):
            state = states[y]
            far, near = p * slope[y], q * slope[y]
            for density in (plane[y] + far, plane[y] + near, plane[y] - near, plane[y] - far):
                state = shade(density, state, sample_count)
            result.append(state)
        return tuple(result)

    zero = jnp.zeros((8, 128), jnp.float32)
    states = lax.fori_loop(0, 16, step, tuple((zero,) * 4 for _ in range(4)))
    for y in range(4):
        opacity, red, green, blue = states[y]
        clear = 1.0 - opacity
        for channel, value in enumerate((red, green, blue, opacity)):
            joined = value + clear * pltpu.roll(value, 4, 0)
            joined = jnp.where(flip > 0, pltpu.roll(joined, 4, 0), joined)
            start = channel * 64 + x * 16 + y * 4
            picture_ref[start : start + 4, :] = joined[0:4]


def kernel(
    sample_count,
    tiles,
    depths,
    coef_ref,
    keep_ref,
    flip_ref,
    out_ref,
    send_ref,
    recv_ref,
    slots_ref,
    picture_ref,
    send2_ref,
    recv2_ref,
    send_sem,
    recv_sem,
    send2_sem,
    recv2_sem,
):
    tile = lax.axis_index("tile")
    depth = lax.axis_index("depth")

    def tile_at(k):
        return (tile // 8 + k // 8) % 4 * 8 + (tile % 8 + k % 8) % 8

    def tile_from(k):
        return (tile // 8 + 4 - k // 8) % 4 * 8 + (tile % 8 + 8 - k % 8) % 8

    barrier = pltpu.get_barrier_semaphore()

    def greet_tile(k, carry):
        pl.semaphore_signal(
            barrier, inc=1, device_id=(tile_at(k), depth), device_id_type=MESH
        )
        return carry

    def greet_depth(k, carry):
        pl.semaphore_signal(
            barrier, inc=1, device_id=(tile, (depth + k) % depths), device_id_type=MESH
        )
        return carry

    lax.fori_loop(1, tiles, greet_tile, 0)
    lax.fori_loop(1, depths, greet_depth, 0)
    pack_strips(coef_ref, keep_ref, send_ref)
    pl.semaphore_wait(barrier, tiles + depths - 2)

    def strip_copy(to, source):
        return pltpu.make_async_remote_copy(
            src_ref=send_ref.at[to],
            dst_ref=recv_ref.at[source],
            send_sem=send_sem.at[to],
            recv_sem=recv_sem.at[source],
            device_id=(to, depth),
            device_id_type=MESH,
        )

    def strip_start(k, carry):
        strip_copy(tile_at(k), tile).start()
        return carry

    def strip_arrive(k, carry):
        strip_copy(tile_at(k), tile_from(k)).wait_recv()
        return carry

    def strip_sent(k, carry):
        strip_copy(tile_at(k), tile).wait_send()
        return carry

    lax.fori_loop(1, tiles, strip_start, 0)
    recv_ref[tile] = send_ref[tile]
    lax.fori_loop(1, tiles, strip_arrive, 0)

    def unpack_step(i, carry):
        unpack_blocks(i, recv_ref, slots_ref)
        return carry

    lax.fori_loop(0, 16, unpack_step, 0)
    flip = flip_ref[0]
    for x in range(4):
        render(x, flip, slots_ref, picture_ref, sample_count)

    for half in range(2):
        turned = picture_ref[128 * half : 128 * half + 128, :].T
        for band in range(16):
            send2_ref[band, half] = turned[8 * band : 8 * band + 8]

    def band_copy(to, source):
        return pltpu.make_async_remote_copy(
            src_ref=send2_ref.at[to],
            dst_ref=recv2_ref.at[source],
            send_sem=send2_sem.at[to],
            recv_sem=recv2_sem.at[source],
            device_id=(tile, to),
            device_id_type=MESH,
        )

    def band_start(k, carry):
        band_copy((depth + k) % depths, depth).start()
        return carry

    def band_arrive(k, carry):
        band_copy((depth + k) % depths, (depth + depths - k) % depths).wait_recv()
        return carry

    def band_sent(k, carry):
        band_copy((depth + k) % depths, depth).wait_send()
        return carry

    lax.fori_loop(1, depths, band_start, 0)
    recv2_ref[depth] = send2_ref[depth]
    lax.fori_loop(1, tiles, strip_sent, 0)
    lax.fori_loop(1, depths, band_arrive, 0)

    lane_high = lax.broadcasted_iota(jnp.int32, (8, 128), 1) >= 64
    passing = jnp.ones((8, 128), jnp.float32)
    total = [jnp.zeros((8, 128), jnp.float32) for _ in range(2)]
    for brick in range(16):
        at = brick + flip * (15 - 2 * brick)
        front, back = recv2_ref[at, 0], recv2_ref[at, 1]
        opacity = jnp.where(lane_high, back, pltpu.roll(back, 64, 1))
        total = [total[0] + passing * front, total[1] + passing * back]
        passing = passing * (1.0 - opacity)
    out_ref[0] = total[0]
    out_ref[1] = total[1]
    lax.fori_loop(1, depths, band_sent, 0)


def per_device(coefficients, keep_count, view_flip):
    tiles, depths = lax.axis_size("tile"), lax.axis_size("depth")
    sample_count = 4 * tiles * depths
    whole = pl.BlockSpec(memory_space=pltpu.VMEM)
    image = pl.pallas_call(
        functools.partial(kernel, sample_count, tiles, depths),
        out_shape=jax.ShapeDtypeStruct((2, 8, 128), jnp.float32),
        in_specs=[whole, whole, pl.BlockSpec(memory_space=pltpu.SMEM)],
        out_specs=whole,
        scratch_shapes=[
            pltpu.VMEM((32, 5, 4, 128), jnp.float32),
            pltpu.VMEM((32, 5, 4, 128), jnp.float32),
            pltpu.VMEM((16, 8, 8, 128), jnp.float32),
            pltpu.VMEM((256, 128), jnp.float32),
            pltpu.VMEM((16, 2, 8, 128), jnp.float32),
            pltpu.VMEM((16, 2, 8, 128), jnp.float32),
            pltpu.SemaphoreType.DMA((32,)),
            pltpu.SemaphoreType.DMA((32,)),
            pltpu.SemaphoreType.DMA((16,)),
            pltpu.SemaphoreType.DMA((16,)),
        ],
        compiler_params=pltpu.CompilerParams(collective_id=0, has_side_effects=True),
    )(coefficients.reshape(8, 128, 128), keep_count.reshape(128, 128), view_flip)
    parts = image.reshape(2, 4, 2, 2, 4, 4, 2, 2)
    return parts.transpose(0, 3, 2, 7, 4, 1, 6, 5).reshape(4, 16, 32)


def solution(mesh):
    placed = (P(None, "depth", "tile", None, None), P("depth", "tile", None, None), P("tile"))
    return jax.shard_map(
        per_device, mesh=mesh, in_specs=placed, out_specs=P(None, "tile", "depth"), check_vma=False
    )
```

time: 86.2 us -> 47.1 us (0.55)
  Pallas kernels: 0 us -> 42 us
  blocking collectives: 22.1 us -> 0 us
  other arithmetic: 20.3 us -> 0 us
  waiting for transfers between devices: 13.9 us -> 0 us
  starting transfers between devices: 10.5 us -> 0 us
  local copies, waits for them, and re-layouts: 14.6 us -> 4.16 us
  matrix products: 3.38 us -> 0 us
    pallas_call x0 -> x1, Pallas kernels: none -> 42 us  [per_device(): pl.pallas_call(functools.partial(kernel, sample_count, tiles, depths), ou...]
    all_to_all x1 -> x0, blocking collectives: 22.1 us -> none  [per_device(): lax.all_to_all(pieces, 'depth', split_axis=2, concat_axis=2, tiled=True)]
    all_to_all x1 -> x0, waiting for transfers between devices: 13.9 us -> none  [per_device(): lax.all_to_all(outgoing, 'tile', split_axis=2, concat_axis=1, tiled=True)]
    reduce_sum x2 -> x0, other arithmetic: 12 us -> none  [the longest x1 11.3 us: render_columns(): red_sum = jnp.sum(weights * jax.nn.sigmoid(2.0 * density), axis=0)]
    all_to_all x1 -> x0, starting transfers between devices: 10.5 us -> none  [per_device(): lax.all_to_all(outgoing, 'tile', split_axis=2, concat_axis=1, tiled=True)]
    unnamed x7 -> x0, local copies, waits for them, and re-layouts: 4.22 us -> none
    another operation x7 -> x0, local copies, waits for them, and re-layouts: 3.48 us -> none  [the longest x2 3.41 us: per_device(): pieces = picture.reshape(4, strip_width, depth_count, band_rows)]
    dot_general x1 -> x0, matrix products: 3.38 us -> none  [render_columns(): jnp.dot(basis_rows, flat_coef, precision=lax.Precision.HIGHEST, preferred...]
  transfers between devices with their start and end apart: 1 -> 0, of which waited for: 1 -> 0; matrix products, arithmetic and copies ran while one was open for 0% -> 0% of each run, Pallas kernels for 0% -> 0%
where the time goes in v1:
time: 47.1 us; the launch traced here: 46.9 us
  Pallas kernels  42 us (89%)
  local copies, waits for them, and re-layouts  4.16 us (9%)
  between operations  0.67 us (1%)
    pallas_call x1, Pallas kernels, per_device(): pl.pallas_call(functools.partial(kernel, sample_count, tiles, depths), ou...  42 us
    transpose x1, local copies, waits for them, and re-layouts, per_device(): return parts.transpose(0, 3, 2, 7, 4, 1, 6, 5).reshape(4, 16, 32)  1.74 us
    reshape x1, local copies, waits for them, and re-layouts, per_device(): parts = image.reshape(2, 4, 2, 2, 4, 4, 2, 2)  1.48 us

profile of v1, /device:TPU:1, one launch (start us, length us, event | category | flops | bytes accessed | tf_op | source)
XLA Modules:
  0.0 46.9 jit_solution(4823096856896220913)
XLA Ops:
  0.7 42.0 %shard_map.37 = f32[2,8,128]{2,1,0:T(8,128)} custom-call(f32[8,128,128]{2,1,0:T(8,128)} %bitcast.4, s32[128,128]{1,0:T(8,128)} %bitcast.5, s32[1]{0:T(128)S(6)} %copy.6.flip_ref), custom_call_target="tpu_custom_call" | custom-call | tf_op jit(solution)/shard_map/pallas_call | solution.py:242
  42.7 1.5 %reshape.14 = f32[2,4,2,2,4,4,2,2]{7,6,5,4,3,2,1,0:T(2,128)S(1)} reshape(f32[2,8,128]{2,1,0:T(8,128)} %shard_map.37) | data formatting | bytes 16384 | tf_op jit(solution)/shard_map/reshape | solution.py:261
  44.2 1.7 %copy.5 = f32[2,2,2,2,4,4,2,4]{7,6,5,4,3,2,1,0:T(2,128)S(1)} copy(f32[2,2,2,2,4,4,2,4]{3,6,7,4,1,2,5,0:T(2,128)S(1)} %bitcast.3) | data formatting | bytes 16384 | tf_op jit(solution)/shard_map/transpose | solution.py:262
  45.9 0.9 %reshape.15 = f32[4,16,32]{2,1,0:T(8,128)} reshape(f32[2,2,2,2,4,4,2,4]{7,6,5,4,3,2,1,0:T(2,128)S(1)} %copy.5) | data formatting | bytes 16384 | tf_op jit(solution)/shard_map/reshape | solution.py:262

commit v2 on v1

--- a/solution.py
+++ b/solution.py
@@ -9,6 +9,7 @@
 from jax.sharding import PartitionSpec as P
 
 MESH = pl.DeviceIdType.MESH
+UNROLL = 4
 LOG2E = math.log2(math.e)
 
 
@@ -96,7 +97,7 @@
         return tuple(result)
 
     zero = jnp.zeros((8, 128), jnp.float32)
-    states = lax.fori_loop(0, 16, step, tuple((zero,) * 4 for _ in range(4)))
+    states = lax.fori_loop(0, 16, step, tuple((zero,) * 4 for _ in range(4)), unroll=UNROLL)
     for y in range(4):
         opacity, red, green, blue = states[y]
         clear = 1.0 - opacity
@@ -119,6 +120,7 @@
     recv_ref,
     slots_ref,
     picture_ref,
+    ordered_ref,
     send2_ref,
     recv2_ref,
     send_sem,
@@ -129,28 +131,18 @@
     tile = lax.axis_index("tile")
     depth = lax.axis_index("depth")
 
-    def tile_at(k):
-        return (tile // 8 + k // 8) % 4 * 8 + (tile % 8 + k % 8) % 8
-
-    def tile_from(k):
-        return (tile // 8 + 4 - k // 8) % 4 * 8 + (tile % 8 + 8 - k % 8) % 8
+    xs = [lax.rem(lax.div(tile, 8) + k, 4) * 8 for k in range(4)]
+    ys = [lax.rem(lax.rem(tile, 8) + k, 8) for k in range(8)]
+    steps = [(dx, dy) for dx in range(4) for dy in range(8)][1:]
+    steps.sort(key=lambda step: -min(step[0], 4 - step[0]) - min(step[1], 8 - step[1]))
+    peers = [xs[dx] + ys[dy] for dx, dy in steps]
+    bands = [lax.rem(depth + k, depths) for k in (8, 7, 9, 6, 10, 5, 11, 4, 12, 3, 13, 2, 14, 1, 15)]
 
     barrier = pltpu.get_barrier_semaphore()
-
-    def greet_tile(k, carry):
-        pl.semaphore_signal(
-            barrier, inc=1, device_id=(tile_at(k), depth), device_id_type=MESH
-        )
-        return carry
-
-    def greet_depth(k, carry):
-        pl.semaphore_signal(
-            barrier, inc=1, device_id=(tile, (depth + k) % depths), device_id_type=MESH
-        )
-        return carry
-
-    lax.fori_loop(1, tiles, greet_tile, 0)
-    lax.fori_loop(1, depths, greet_depth, 0)
+    for to in peers:
+        pl.semaphore_signal(barrier, inc=1, device_id=(to, depth), device_id_type=MESH)
+    for to in bands:
+        pl.semaphore_signal(barrier, inc=1, device_id=(tile, to), device_id_type=MESH)
     pack_strips(coef_ref, keep_ref, send_ref)
     pl.semaphore_wait(barrier, tiles + depths - 2)
 
@@ -164,21 +156,11 @@
             device_id_type=MESH,
         )
 
-    def strip_start(k, carry):
-        strip_copy(tile_at(k), tile).start()
-        return carry
-
-    def strip_arrive(k, carry):
-        strip_copy(tile_at(k), tile_from(k)).wait_recv()
-        return carry
-
-    def strip_sent(k, carry):
-        strip_copy(tile_at(k), tile).wait_send()
-        return carry
-
-    lax.fori_loop(1, tiles, strip_start, 0)
+    for to in peers:
+        strip_copy(to, tile).start()
     recv_ref[tile] = send_ref[tile]
-    lax.fori_loop(1, tiles, strip_arrive, 0)
+    for source in peers:
+        strip_copy(source, source).wait_recv()
 
     def unpack_step(i, carry):
         unpack_blocks(i, recv_ref, slots_ref)
@@ -189,8 +171,16 @@
     for x in range(4):
         render(x, flip, slots_ref, picture_ref, sample_count)
 
+    for channel in range(4):
+        for x in range(4):
+            for column in range(2):
+                for block in range(2):
+                    source = channel * 64 + x * 16 + block * 2 + column
+                    start = channel * 64 + (7 - column * 4 - x) * 8 + block * 4
+                    ordered_ref[start : start + 4, :] = picture_ref[pl.ds(source, 4, stride=4), :]
+
     for half in range(2):
-        turned = picture_ref[128 * half : 128 * half + 128, :].T
+        turned = ordered_ref[128 * half : 128 * half + 128, :].T
         for band in range(16):
             send2_ref[band, half] = turned[8 * band : 8 * band + 8]
 
@@ -204,22 +194,13 @@
             device_id_type=MESH,
         )
 
-    def band_start(k, carry):
-        band_copy((depth + k) % depths, depth).start()
-        return carry
-
-    def band_arrive(k, carry):
-        band_copy((depth + k) % depths, (depth + depths - k) % depths).wait_recv()
-        return carry
-
-    def band_sent(k, carry):
-        band_copy((depth + k) % depths, depth).wait_send()
-        return carry
-
-    lax.fori_loop(1, depths, band_start, 0)
+    for to in bands:
+        band_copy(to, depth).start()
     recv2_ref[depth] = send2_ref[depth]
-    lax.fori_loop(1, tiles, strip_sent, 0)
-    lax.fori_loop(1, depths, band_arrive, 0)
+    for to in peers:
+        strip_copy(to, tile).wait_send()
+    for source in bands:
+        band_copy(source, source).wait_recv()
 
     lane_high = lax.broadcasted_iota(jnp.int32, (8, 128), 1) >= 64
     passing = jnp.ones((8, 128), jnp.float32)
@@ -230,24 +211,36 @@
         opacity = jnp.where(lane_high, back, pltpu.roll(back, 64, 1))
         total = [total[0] + passing * front, total[1] + passing * back]
         passing = passing * (1.0 - opacity)
-    out_ref[0] = total[0]
-    out_ref[1] = total[1]
-    lax.fori_loop(1, depths, band_sent, 0)
+    lane_pair = lax.broadcasted_iota(jnp.int32, (8, 128), 1) // 8
+    for channel in range(4):
+        values = [jnp.zeros((8, 128), jnp.float32)] * 2
+        for pair in range(4):
+            shift = (8 * pair - 64 * (channel % 2) - 56) % 128
+            moved = pltpu.roll(total[channel // 2], shift, 1)
+            for half in range(2):
+                row = jnp.broadcast_to(moved[2 * pair + half : 2 * pair + half + 1], (8, 128))
+                spread = pltpu.roll(row, 0, 1, stride=8, stride_axis=0)
+                values[half] = jnp.where(lane_pair == pair, spread, values[half])
+        for half in range(2):
+            out_ref[channel, 8 * half : 8 * half + 8, :] = values[half][:, :32]
+    for to in bands:
+        band_copy(to, depth).wait_send()
 
 
 def per_device(coefficients, keep_count, view_flip):
     tiles, depths = lax.axis_size("tile"), lax.axis_size("depth")
     sample_count = 4 * tiles * depths
     whole = pl.BlockSpec(memory_space=pltpu.VMEM)
-    image = pl.pallas_call(
+    return pl.pallas_call(
         functools.partial(kernel, sample_count, tiles, depths),
-        out_shape=jax.ShapeDtypeStruct((2, 8, 128), jnp.float32),
+        out_shape=jax.ShapeDtypeStruct((4, 16, 32), jnp.float32),
         in_specs=[whole, whole, pl.BlockSpec(memory_space=pltpu.SMEM)],
         out_specs=whole,
         scratch_shapes=[
             pltpu.VMEM((32, 5, 4, 128), jnp.float32),
             pltpu.VMEM((32, 5, 4, 128), jnp.float32),
             pltpu.VMEM((16, 8, 8, 128), jnp.float32),
+            pltpu.VMEM((256, 128), jnp.float32),
             pltpu.VMEM((256, 128), jnp.float32),
             pltpu.VMEM((16, 2, 8, 128), jnp.float32),
             pltpu.VMEM((16, 2, 8, 128), jnp.float32),
@@ -258,8 +251,6 @@
         ],
         compiler_params=pltpu.CompilerParams(collective_id=0, has_side_effects=True),
     )(coefficients.reshape(8, 128, 128), keep_count.reshape(128, 128), view_flip)
-    parts = image.reshape(2, 4, 2, 2, 4, 4, 2, 2)
-    return parts.transpose(0, 3, 2, 7, 4, 1, 6, 5).reshape(4, 16, 32)
 
 
 def solution(mesh):

time: 47.1 us -> 41.6 us (0.88)
  local copies, waits for them, and re-layouts: 4.16 us -> 1.38 us
  Pallas kernels: 42 us -> 39.3 us
    pallas_call x1, Pallas kernels: 42 us -> 39.3 us  [per_device(): pl.pallas_call(functools.partial(kernel, sample_count, tiles, depths), ou...]
    reshape x2 -> x0, local copies, waits for them, and re-layouts: 2.42 us -> none  [the longest x1 1.48 us: per_device(): parts = image.reshape(2, 4, 2, 2, 4, 4, 2, 2)]
    transpose x1 -> x0, local copies, waits for them, and re-layouts: 1.74 us -> none  [per_device(): return parts.transpose(0, 3, 2, 7, 4, 1, 6, 5).reshape(4, 16, 32)]
    unnamed x0 -> x1, local copies, waits for them, and re-layouts: none -> 1.38 us
where the time goes in v2:
time: 41.6 us; the launch traced here: 41.4 us
  Pallas kernels  39.3 us (94%)
  local copies, waits for them, and re-layouts  1.38 us (3%)
  between operations  0.66 us (2%)
    pallas_call x1, Pallas kernels, per_device(): pl.pallas_call(functools.partial(kernel, sample_count, tiles, depths), ou...  39.3 us
    unnamed x1, local copies, waits for them, and re-layouts  1.38 us

profile of v2, /device:TPU:1, one launch (start us, length us, event | category | flops | bytes accessed | tf_op | source)
XLA Modules:
  0.0 41.4 jit_solution(14134021397609418783)
XLA Ops:
  0.7 39.3 %shard_map.37 = f32[4,16,32]{2,1,0:T(8,128)} custom-call(f32[8,128,128]{2,1,0:T(8,128)} %bitcast.2, s32[128,128]{1,0:T(8,128)} %bitcast.3, s32[1]{0:T(128)S(6)} %copy.5.flip_ref), custom_call_target="tpu_custom_call" | custom-call | tf_op jit(solution)/shard_map/pallas_call | solution.py:234
  40.0 1.4 %copy.6 = f32[4,16,32]{2,1,0:T(8,128)} copy(f32[4,16,32]{2,1,0:T(8,128)} %shard_map.37) | data formatting | bytes 16384

commit v3 on v2

v3 whole, which is shorter than its diff:
```python
import functools
import math

import jax
import jax.numpy as jnp
from jax import lax
from jax.experimental import pallas as pl
from jax.experimental.pallas import tpu as pltpu
from jax.sharding import PartitionSpec as P

MESH = pl.DeviceIdType.MESH
UNROLL = 4
LOG2E = math.log2(math.e)


def cosine(frequency, position):
    factor = 0.5 if frequency == 0 else math.sqrt(0.5)
    return factor * math.cos(math.pi * (2 * position + 1) * frequency / 8.0)


def pack_strips(coef_ref, keep_ref, send_ref):
    lane_even = lax.broadcasted_iota(jnp.int32, (8, 128), 1) % 2 == 0
    row_low = lax.broadcasted_iota(jnp.int32, (8, 128), 0) % 2 == 0
    for group in range(16):
        rows = slice(8 * group, 8 * group + 8)
        count = keep_ref[rows, :]
        first = [coef_ref[k, rows, :] for k in range(8)]
        second = [pltpu.roll(value, 127, 1) for value in first]
        packed = [first[0]]
        packed += [jnp.where(count > k, first[k], second[8 - k]) for k in range(1, 8)]
        packed += [second[0], count.astype(jnp.float32)]
        for q in range(5):
            low, high = packed[2 * q], packed[2 * q + 1]
            own = jnp.where(row_low, low, pltpu.roll(high, 1, 0))
            other = jnp.where(row_low, pltpu.roll(low, 7, 0), high)
            merged = jnp.where(lane_even, own, pltpu.roll(other, 1, 1))
            for part in range(4):
                send_ref[part % 2, 2 * group + part // 2, q] = merged[2 * part : 2 * part + 2]


def unpack_blocks(half, i, recv_ref, slots_ref):
    row_low = lax.broadcasted_iota(jnp.int32, (8, 128), 0) % 2 == 0
    tiles = [
        jnp.concatenate([recv_ref[half, 8 * segment + i, q] for segment in range(4)], axis=0)
        for q in range(5)
    ]
    down = [pltpu.roll(value, 1, 0) for value in tiles]
    up = [pltpu.roll(value, 7, 0) for value in tiles]
    count = jnp.where(row_low, up[4], tiles[4])
    kept = jnp.where(row_low, count, 9.0 - count)
    for k in range(8):
        if k % 2 == 0:
            value = jnp.where(row_low, tiles[k // 2], down[(8 - k) // 2])
        else:
            value = jnp.where(row_low, up[k // 2], tiles[(7 - k) // 2])
        if k > 0:
            value = jnp.where(kept > k, value, 0.0)
        slots_ref[i, k] = value


def shade(density, state, sample_count):
    opacity, red, green, blue = state
    u = jnp.exp2(density)
    third = u * (LOG2E - u * (LOG2E / 2 - u * (LOG2E / 3)))
    soft = jnp.where(u < 2.0**-8, third, jnp.log2(1.0 + u))
    t = 1.5 * math.log(2.0) / sample_count
    alpha = soft * (t - soft * (t**2 / 2 - soft * (t**3 / 6 - soft * (t**4 / 24))))
    weight = (1.0 - opacity) * alpha
    v = jnp.exp2(0.5 * density - 1.5 * LOG2E)
    red = red + weight * jnp.exp2(density - soft)
    green = green + weight * jnp.exp2(density * density * (-1.0 / (4 * LOG2E)))
    blue = blue + weight * jnp.exp2(-jnp.log2(1.0 + v))
    return opacity + weight, red, green, blue


def render(x, flip, slots_ref, picture_ref, sample_count):
    unit = 2 * LOG2E
    c0 = cosine(0, 0)
    b1x, b2x = cosine(1, x), cosine(2, x)
    p, q, h = cosine(1, 0), cosine(1, 1), cosine(2, 0)
    turn = (1 - 2 * flip).astype(jnp.float32)

    def step(i, states):
        at = i + flip * (7 - 2 * i)
        a = [slots_ref[at, k] for k in range(8)]
        base = (unit * c0**3) * a[0] + (unit * c0**2 * b1x) * a[2] + (unit * c0**2 * b2x) * a[6]
        along = (unit * c0**2) * a[1] + (unit * c0 * b1x) * a[5]
        curve = (unit * c0**2 * h) * a[4]
        deep, tilt = (unit * c0**2 * turn) * a[3], (unit * c0 * turn) * a[7]
        outer, inner = base + curve, base - curve
        plane = [outer + p * along, inner + q * along, inner - q * along, outer - p * along]
        slope = [deep + p * tilt, deep + q * tilt, deep - q * tilt, deep - p * tilt]
        result = []
        for y in range(4):
            state = states[y]
            far, near = p * slope[y], q * slope[y]
            for density in (plane[y] + far, plane[y] + near, plane[y] - near, plane[y] - far):
                state = shade(density, state, sample_count)
            result.append(state)
        return tuple(result)

    zero = jnp.zeros((8, 128), jnp.float32)
    states = lax.fori_loop(0, 8, step, tuple((zero,) * 4 for _ in range(4)), unroll=UNROLL)
    for y in range(4):
        opacity, red, green, blue = states[y]
        values = [red, green, blue, opacity]
        for distance in (2, 4):
            clear = 1.0 - values[3]
            if distance == 2:
                beyond = [
                    jnp.where(flip > 0, pltpu.roll(value, 2, 0), pltpu.roll(value, 6, 0))
                    for value in values
                ]
            else:
                beyond = [pltpu.roll(value, 4, 0) for value in values]
            values = [value + clear * more for value, more in zip(values, beyond)]
        for channel, value in enumerate(values):
            value = jnp.where(flip > 0, pltpu.roll(value, 2, 0), value)
            start = channel * 32 + x * 8 + y * 2
            picture_ref[start : start + 2, :] = value[0:2]


def kernel(
    sample_count,
    tiles,
    depths,
    coef_ref,
    keep_ref,
    flip_ref,
    out_ref,
    send_ref,
    recv_ref,
    slots_ref,
    picture_ref,
    ordered_ref,
    send2_ref,
    recv2_first,
    recv2_second,
    send_sem,
    recv_sem,
    send2_sem,
    recv2_sem,
):
    tile = lax.axis_index("tile")
    depth = lax.axis_index("depth")
    recv2 = (recv2_first, recv2_second)

    xs = [lax.rem(lax.div(tile, 8) + k, 4) * 8 for k in range(4)]
    ys = [lax.rem(lax.rem(tile, 8) + k, 8) for k in range(8)]
    steps = [(dx, dy) for dx in range(4) for dy in range(8)][1:]
    steps.sort(key=lambda step: -min(step[0], 4 - step[0]) - min(step[1], 8 - step[1]))
    peers = [xs[dx] + ys[dy] for dx, dy in steps]
    bands = [lax.rem(depth + k, depths) for k in (8, 7, 9, 6, 10, 5, 11, 4, 12, 3, 13, 2, 14, 1, 15)]

    barrier = pltpu.get_barrier_semaphore()
    for to in peers:
        pl.semaphore_signal(barrier, inc=1, device_id=(to, depth), device_id_type=MESH)
    for to in bands:
        pl.semaphore_signal(barrier, inc=1, device_id=(tile, to), device_id_type=MESH)
    pack_strips(coef_ref, keep_ref, send_ref)
    pl.semaphore_wait(barrier, tiles + depths - 2)

    def strip_copy(half, to, source):
        return pltpu.make_async_remote_copy(
            src_ref=send_ref.at[half, to],
            dst_ref=recv_ref.at[half, source],
            send_sem=send_sem.at[half, to],
            recv_sem=recv_sem.at[half, source],
            device_id=(to, depth),
            device_id_type=MESH,
        )

    def band_copy(half, to, source):
        return pltpu.make_async_remote_copy(
            src_ref=send2_ref.at[half, to],
            dst_ref=recv2[half].at[source],
            send_sem=send2_sem.at[half, to],
            recv_sem=recv2_sem.at[half, source],
            device_id=(tile, to),
            device_id_type=MESH,
        )

    for half in range(2):
        for to in peers:
            strip_copy(half, to, tile).start()
        recv_ref[half, tile] = send_ref[half, tile]

    flip = flip_ref[0]
    for half in range(2):
        for source in peers:
            strip_copy(half, source, source).wait_recv()

        def unpack_step(i, carry):
            unpack_blocks(half, i, recv_ref, slots_ref)
            return carry

        lax.fori_loop(0, 8, unpack_step, 0)
        for x in range(4):
            render(x, flip, slots_ref, picture_ref, sample_count)
        for channel in range(4):
            for x in range(4):
                for block in range(2):
                    source = channel * 32 + x * 8 + block
                    start = channel * 32 + (3 - x) * 8 + block * 4
                    ordered_ref[start : start + 4, :] = picture_ref[pl.ds(source, 4, stride=2), :]
        turned = ordered_ref[...].T
        for band in range(16):
            send2_ref[half, band] = turned[8 * band : 8 * band + 8]
        for to in bands:
            band_copy(half, to, depth).start()
        recv2[half][depth] = send2_ref[half, depth]

    for half in range(2):
        for to in peers:
            strip_copy(half, to, tile).wait_send()
    lane = lax.broadcasted_iota(jnp.int32, (8, 128), 1)
    row_first = lax.broadcasted_iota(jnp.int32, (8, 128), 0) < 4
    for half in range(2):
        for source in bands:
            band_copy(half, source, source).wait_recv()
        passing = jnp.ones((8, 128), jnp.float32)
        total = jnp.zeros((8, 128), jnp.float32)
        for brick in range(16):
            front = recv2[half][brick + flip * (15 - 2 * brick)]
            opacity = jnp.where(lane >= 96, front, pltpu.roll(front, 64, 1))
            opacity = jnp.where(lane // 32 % 2 == 1, opacity, pltpu.roll(opacity, 32, 1))
            total = total + passing * front
            passing = passing * (1.0 - opacity)
        for channel in range(4):
            value = jnp.zeros((8, 128), jnp.float32)
            for pair in range(4):
                shift = 8 * pair - 32 * channel - 24
                first = pltpu.roll(total, shift % 128, 1)[2 * pair : 2 * pair + 1]
                second = pltpu.roll(total, (shift - 32) % 128, 1)[2 * pair + 1 : 2 * pair + 2]
                rows = jnp.where(
                    row_first, jnp.broadcast_to(first, (8, 128)), jnp.broadcast_to(second, (8, 128))
                )
                spread = pltpu.roll(rows, 0, 1, stride=8, stride_axis=0)
                value = jnp.where(lane // 8 == pair, spread, value)
            out_ref[channel, 8 * half : 8 * half + 8, :] = value[:, :32]
    for half in range(2):
        for to in bands:
            band_copy(half, to, depth).wait_send()


def per_device(coefficients, keep_count, view_flip):
    tiles, depths = lax.axis_size("tile"), lax.axis_size("depth")
    sample_count = 4 * tiles * depths
    whole = pl.BlockSpec(memory_space=pltpu.VMEM)
    return pl.pallas_call(
        functools.partial(kernel, sample_count, tiles, depths),
        out_shape=jax.ShapeDtypeStruct((4, 16, 32), jnp.float32),
        in_specs=[whole, whole, pl.BlockSpec(memory_space=pltpu.SMEM)],
        out_specs=whole,
        scratch_shapes=[
            pltpu.VMEM((2, 32, 5, 2, 128), jnp.float32),
            pltpu.VMEM((2, 32, 5, 2, 128), jnp.float32),
            pltpu.VMEM((8, 8, 8, 128), jnp.float32),
            pltpu.VMEM((128, 128), jnp.float32),
            pltpu.VMEM((128, 128), jnp.float32),
            pltpu.VMEM((2, 16, 8, 128), jnp.float32),
            pltpu.VMEM((16, 8, 128), jnp.float32),
            pltpu.VMEM((16, 8, 128), jnp.float32),
            pltpu.SemaphoreType.DMA((2, 32)),
            pltpu.SemaphoreType.DMA((2, 32)),
            pltpu.SemaphoreType.DMA((2, 16)),
            pltpu.SemaphoreType.DMA((2, 16)),
        ],
        compiler_params=pltpu.CompilerParams(collective_id=0, has_side_effects=True),
    )(coefficients.reshape(8, 128, 128), keep_count.reshape(128, 128), view_flip)


def solution(mesh):
    placed = (P(None, "depth", "tile", None, None), P("depth", "tile", None, None), P("tile"))
    return jax.shard_map(
        per_device, mesh=mesh, in_specs=placed, out_specs=P(None, "tile", "depth"), check_vma=False
    )
```

time: 41.6 us -> 39.9 us (0.959)
  Pallas kernels: 39.3 us -> 37.6 us
    pallas_call x1, Pallas kernels: 39.3 us -> 37.6 us  [per_device(): pl.pallas_call(functools.partial(kernel, sample_count, tiles, depths), ou...]
where the time goes in v3:
time: 39.9 us; the launch traced here: 39.7 us
  Pallas kernels  37.6 us (94%)
  local copies, waits for them, and re-layouts  1.38 us (3%)
  between operations  0.66 us (2%)
    pallas_call x1, Pallas kernels, per_device(): pl.pallas_call(functools.partial(kernel, sample_count, tiles, depths), ou...  37.6 us
    unnamed x1, local copies, waits for them, and re-layouts  1.38 us

profile of v3, /device:TPU:1, one launch (start us, length us, event | category | flops | bytes accessed | tf_op | source)
XLA Modules:
  0.0 39.7 jit_solution(11200346604799304723)
XLA Ops:
  0.7 37.6 %shard_map.37 = f32[4,16,32]{2,1,0:T(8,128)} custom-call(f32[8,128,128]{2,1,0:T(8,128)} %bitcast.2, s32[128,128]{1,0:T(8,128)} %bitcast.3, s32[1]{0:T(128)S(6)} %copy.5.flip_ref), custom_call_target="tpu_custom_call" | custom-call | tf_op jit(solution)/shard_map/pallas_call | solution.py:250
  38.3 1.4 %copy.6 = f32[4,16,32]{2,1,0:T(8,128)} copy(f32[4,16,32]{2,1,0:T(8,128)} %shard_map.37) | data formatting | bytes 16384

commit v4 on v3

--- a/solution.py
+++ b/solution.py
@@ -124,10 +124,14 @@
     sample_count,
     tiles,
     depths,
+    coef_hbm,
+    keep_hbm,
+    flip_ref,
+    out_ref,
     coef_ref,
     keep_ref,
-    flip_ref,
-    out_ref,
+    coef_sem,
+    keep_sem,
     send_ref,
     recv_ref,
     slots_ref,
@@ -141,6 +145,12 @@
     send2_sem,
     recv2_sem,
 ):
+    loads = [
+        pltpu.make_async_copy(coef_hbm, coef_ref, coef_sem),
+        pltpu.make_async_copy(keep_hbm, keep_ref, keep_sem),
+    ]
+    for load in loads:
+        load.start()
     tile = lax.axis_index("tile")
     depth = lax.axis_index("depth")
     recv2 = (recv2_first, recv2_second)
@@ -157,6 +167,8 @@
         pl.semaphore_signal(barrier, inc=1, device_id=(to, depth), device_id_type=MESH)
     for to in bands:
         pl.semaphore_signal(barrier, inc=1, device_id=(tile, to), device_id_type=MESH)
+    for load in loads:
+        load.wait()
     pack_strips(coef_ref, keep_ref, send_ref)
     pl.semaphore_wait(barrier, tiles + depths - 2)
 
@@ -247,12 +259,17 @@
     tiles, depths = lax.axis_size("tile"), lax.axis_size("depth")
     sample_count = 4 * tiles * depths
     whole = pl.BlockSpec(memory_space=pltpu.VMEM)
+    far = pl.BlockSpec(memory_space=pltpu.HBM)
     return pl.pallas_call(
         functools.partial(kernel, sample_count, tiles, depths),
         out_shape=jax.ShapeDtypeStruct((4, 16, 32), jnp.float32),
-        in_specs=[whole, whole, pl.BlockSpec(memory_space=pltpu.SMEM)],
+        in_specs=[far, far, pl.BlockSpec(memory_space=pltpu.SMEM)],
         out_specs=whole,
         scratch_shapes=[
+            pltpu.VMEM((8, 128, 128), jnp.float32),
+            pltpu.VMEM((128, 128), jnp.int32),
+            pltpu.SemaphoreType.DMA,
+            pltpu.SemaphoreType.DMA,
             pltpu.VMEM((2, 32, 5, 2, 128), jnp.float32),
             pltpu.VMEM((2, 32, 5, 2, 128), jnp.float32),
             pltpu.VMEM((8, 8, 8, 128), jnp.float32),

time: 39.9 us -> 38.8 us (0.972)
  Pallas kernels: 37.6 us -> 36.6 us
    pallas_call x1, Pallas kernels: 37.6 us -> 36.6 us  [per_device(): pl.pallas_call(functools.partial(kernel, sample_count, tiles, depths), ou...]
where the time goes in v4:
time: 38.8 us; the launch traced here: 38.6 us
  Pallas kernels  36.6 us (94%)
  local copies, waits for them, and re-layouts  1.38 us (4%)
  between operations  0.66 us (2%)
    pallas_call x1, Pallas kernels, per_device(): pl.pallas_call(functools.partial(kernel, sample_count, tiles, depths), ou...  36.6 us
    unnamed x1, local copies, waits for them, and re-layouts  1.38 us

profile of v4, /device:TPU:1, one launch (start us, length us, event | category | flops | bytes accessed | tf_op | source)
XLA Modules:
  0.0 38.6 jit_solution(7571018534062774912)
XLA Ops:
  0.7 36.6 %shard_map.37 = f32[4,16,32]{2,1,0:T(8,128)} custom-call(f32[8,128,128]{2,1,0:T(8,128)} %bitcast.2, s32[128,128]{1,0:T(8,128)} %bitcast.3, s32[1]{0:T(128)S(6)} %copy.5.flip_ref), custom_call_target="tpu_custom_call" | custom-call | tf_op jit(solution)/shard_map/pallas_call | solution.py:263
  37.2 1.4 %copy.6 = f32[4,16,32]{2,1,0:T(8,128)} copy(f32[4,16,32]{2,1,0:T(8,128)} %shard_map.37) | data formatting | bytes 16384

commit v5 on v4

--- a/solution.py
+++ b/solution.py
@@ -9,7 +9,7 @@
 from jax.sharding import PartitionSpec as P
 
 MESH = pl.DeviceIdType.MESH
-UNROLL = 4
+UNROLL = 8
 LOG2E = math.log2(math.e)
 
 

time: 38.8 us -> 38.6 us (level)
  no operation moved by 1% of the time
where the time goes in v5:
time: 38.6 us; the launch traced here: 38.4 us
  Pallas kernels  36.3 us (94%)
  local copies, waits for them, and re-layouts  1.38 us (4%)
  between operations  0.66 us (2%)
    pallas_call x1, Pallas kernels, per_device(): pl.pallas_call(functools.partial(kernel, sample_count, tiles, depths), ou...  36.3 us
    unnamed x1, local copies, waits for them, and re-layouts  1.38 us

profile of v5, /device:TPU:1, one launch (start us, length us, event | category | flops | bytes accessed | tf_op | source)
XLA Modules:
  0.0 38.4 jit_solution(10461434482523211541)
XLA Ops:
  0.7 36.3 %shard_map.37 = f32[4,16,32]{2,1,0:T(8,128)} custom-call(f32[8,128,128]{2,1,0:T(8,128)} %bitcast.2, s32[128,128]{1,0:T(8,128)} %bitcast.3, s32[1]{0:T(128)S(6)} %copy.5.flip_ref), custom_call_target="tpu_custom_call" | custom-call | tf_op jit(solution)/shard_map/pallas_call | solution.py:263
  37.0 1.4 %copy.6 = f32[4,16,32]{2,1,0:T(8,128)} copy(f32[4,16,32]{2,1,0:T(8,128)} %shard_map.37) | data formatting | bytes 16384
